TPU v7x, 32 devices: a whole 2x2x4 slice. The times are simulated.
32 devices in a mesh: groups: 2 (over y), seq: 8 (over z, x), vocab: 2 (over core).
Axes of the slice: x: 2, y: 2, z: 4, core: 2. Of those that a mesh axis runs over, the one named last changes fastest.
Arguments:
- ssm_input: bfloat16 [128, 2560], P(('groups', 'seq'), 'vocab'), parts along dimension 0, may hold values from -6 to 6
- gate_input: bfloat16 [128, 2560], P(('groups', 'seq'), 'vocab'), parts along dimension 0, may hold values from -6 to 6
- b_proj: bfloat16 [128, 128], P(('groups', 'seq')), parts along dimension 0, may hold values from -1.796875 to 1.796875
- readout_matrix: bfloat16 [128, 128], P(('groups', 'seq')), parts along dimension 0, may hold values from -1.796875 to 1.796875
- step_raw: float32 [128, 40], P(('groups', 'seq'), 'vocab'), parts along dimension 0, may hold values from -3 to 7
- step_bias: float32 [40], P('vocab'), may hold values from -1 to 1
- decay_log: float32 [40], P('vocab'), may hold values from -9 to -2
- head_skip_gain: float32 [40], P('vocab'), may hold values from 0.5 to 1.5
- norm_gain: float32 [2560], P('vocab'), may hold values from 0.1 to 1.9
- out_weight: bfloat16 [2560, 2560], P('vocab', 'seq'), may hold values from -0.125 to 0.125
- residual: bfloat16 [128, 2560], P('groups', 'seq'), parts along dimension 0, may hold values from -6 to 6
- final_gain: float32 [2560], replicated, may hold values from 0.1 to 1.9
- head_weight: bfloat16 [2560, 3136], P(None, ('seq', 'vocab')), may hold values from -12.253826 to 12.253826
- mask_table: int32 [96, 3136], P(None, ('seq', 'vocab')), may hold values 0 or 1
- state_ids: int32 [128], P(('groups', 'seq')), parts along dimension 0, may hold values from 0 to 95
- targets: int32 [128], P(('groups', 'seq')), parts along dimension 0, may hold values from 0 to 3135
Outputs:
- token_nll_loss: float32 [128], P(('groups', 'seq', 'vocab')), parts along dimension 0
There are 2 independent parts, one for each index of `groups`. A program takes and returns all parts, laid end to end along the dimension named above; an argument that names none is the same for every part. Nothing has to cross between parts.
All inputs are finite; a program needn't handle non-finite values. No bound on the sum of `mask_table` on one device may be relied on, other than what follows from the above.
Results may differ from a plain program's by a relative error of at most 0.0022.
Values may be sent and summed in bfloat16 or wider, within the bound.
No kernel may reach another device: no remote copies, remote signals or barrier semaphores. Data moves between devices by JAX's collectives and lax.ppermute only.
A program may use at most 192 MiB of HBM per device.

v0:
```python
import jax
import jax.numpy as jnp
from jax import lax
from jax.sharding import PartitionSpec as P


def carried_in(value, axis, join, neutral):
    count, mine = (lax.axis_size(axis), lax.axis_index(axis))
    pieces = jax.tree.map(lambda part: lax.all_gather(part, axis), value)
    total = jax.tree.map(
        lambda part, zero: jnp.full_like(part, 0) + jnp.asarray(zero, part.dtype), value, neutral
    )

    def lap(position, total):
        longer = join(total, jax.tree.map(lambda part: part[position], pieces))
        return jax.tree.map(lambda new, old: jnp.where(position < mine, new, old), longer, total)

    return lax.fori_loop(0, count - 1, lap, total)


def joined(part, axis, combine):
    gathered = jax.tree.map(lambda a: lax.all_gather(a, axis), part)

    def take(source):
        return jax.tree.map(lambda a: lax.dynamic_index_in_dim(a, source, 0, False), gathered)

    return lax.fori_loop(
        1, lax.axis_size(axis), lambda source, state: combine(state, take(source)), take(0)
    )


def carry_join(preceding, later):
    return (preceding[0] * later[0], preceding[1] * later[0][:, None, None] + later[1])


def total_join(first, second):
    top = jnp.maximum(first[0], second[0])
    total = first[1] * jnp.exp(first[0] - top) + second[1] * jnp.exp(second[0] - top)
    return (top, total, first[2] + second[2])


def shards(
    ssm_input,
    gate_input,
    b_proj,
    readout_matrix,
    step_raw,
    step_bias,
    decay_log,
    head_skip_gain,
    norm_gain,
    out_weight,
    residual,
    final_gain,
    head_weight,
    mask_table,
    state_ids,
    targets,
):
    highest = lax.Precision.HIGHEST
    rows = ssm_input.shape[0]
    heads = step_raw.shape[1]
    channels = ssm_input.shape[1]
    head_size = channels // heads
    state_size = b_proj.shape[1]
    step = jax.nn.softplus(step_raw + step_bias[None, :])
    log_rate = step * -jnp.exp(decay_log)[None, :]
    log_cum = jnp.cumsum(log_rate, axis=0)
    values = ssm_input.astype(jnp.float32).reshape(rows, heads, head_size)
    scaled = values * step[:, :, None]
    in_rows = b_proj.astype(jnp.float32)
    out_rows = readout_matrix.astype(jnp.float32)
    correlations = jnp.dot(out_rows, in_rows.T, precision=highest)
    causal = jnp.arange(rows)[:, None] >= jnp.arange(rows)[None, :]
    spread = log_cum[:, None, :] - log_cum[None, :, :]
    weights = jnp.exp(jnp.where(causal[:, :, None], spread, -1e30))
    within = jnp.einsum("tsh,ts,shp->thp", weights, correlations, scaled, precision=highest)
    last_log = log_cum[rows - 1]
    tails = jnp.exp(last_log[None, :] - log_cum)
    local_state = jnp.einsum("sh,shp,sn->hpn", tails, scaled, in_rows, precision=highest)
    identity = (
        jnp.ones((heads,), jnp.float32),
        jnp.zeros((heads, head_size, state_size), jnp.float32),
    )
    _, incoming = carried_in((jnp.exp(last_log), local_state), "seq", carry_join, identity)
    carried = jnp.einsum("th,hpn,tn->thp", jnp.exp(log_cum), incoming, out_rows, precision=highest)
    mixed = within + carried + head_skip_gain[None, :, None] * values
    gated = (mixed.reshape(rows, channels) * jax.nn.silu(gate_input.astype(jnp.float32))).astype(
        jnp.bfloat16
    )
    every_rows, all_states, all_targets = (
        lax.all_gather(gated, "seq", axis=0, tiled=True),
        lax.all_gather(state_ids, "seq", axis=0, tiled=True),
        lax.all_gather(targets, "seq", axis=0, tiled=True),
    )
    every_f = every_rows.astype(jnp.float32)
    squares = lax.psum(jnp.sum(every_f * every_f, axis=-1), "vocab")
    pair_count = lax.axis_size("vocab")
    scale = lax.rsqrt(squares / (channels * pair_count) + 1e-05)
    normed = (every_f * scale[:, None] * norm_gain[None, :]).astype(jnp.bfloat16)
    partial_sum = jnp.dot(normed, out_weight, preferred_element_type=jnp.float32)
    summed = lax.psum(partial_sum, "vocab")
    hidden = (residual.astype(jnp.float32) + summed).astype(jnp.bfloat16)
    full = lax.all_gather(hidden, "seq", axis=1, tiled=True)
    full_f = full.astype(jnp.float32)
    scale_two = lax.rsqrt(jnp.mean(full_f * full_f, axis=-1) + 1e-05)
    final = (full_f * scale_two[:, None] * final_gain[None, :]).astype(jnp.bfloat16)
    vocab_logits = jnp.dot(final, head_weight, preferred_element_type=jnp.float32)
    entries = head_weight.shape[1]
    block_index = lax.axis_index("seq") * pair_count + lax.axis_index("vocab")
    vocab_ids = block_index * entries + jnp.arange(entries, dtype=jnp.int32)
    state_count = mask_table.shape[0]
    one_hot = (all_states[:, None] == jnp.arange(state_count, dtype=jnp.int32)[None, :]).astype(
        jnp.float32
    )
    table_rows = jnp.dot(one_hot, mask_table.astype(jnp.float32))
    is_target = vocab_ids[None, :] == all_targets[:, None]
    allowed = (table_rows > 0.5) | is_target
    local_top = jnp.max(jnp.where(allowed, vocab_logits, -1e30), axis=-1)
    local_total = jnp.sum(
        jnp.where(allowed, jnp.exp(vocab_logits - local_top[:, None]), 0.0), axis=-1
    )
    local_pick = jnp.sum(jnp.where(is_target, vocab_logits, 0.0), axis=-1)
    positions = vocab_logits.shape[0]
    seq_count = lax.axis_size("seq")
    own_rows = positions // (seq_count * pair_count)
    top, total, picked = joined((local_top, local_total, local_pick), ("seq", "vocab"), total_join)
    losses = jnp.log(total) + top - picked
    return lax.dynamic_slice_in_dim(losses, block_index * own_rows, own_rows, 0)


def solution(mesh):
    placed = (
        P(("groups", "seq"), "vocab"),
        P(("groups", "seq"), "vocab"),
        P(("groups", "seq"), None),
        P(("groups", "seq"), None),
        P(("groups", "seq"), "vocab"),
        P("vocab"),
        P("vocab"),
        P("vocab"),
        P("vocab"),
        P("vocab", "seq"),
        P("groups", "seq"),
        P(),
        P(None, ("seq", "vocab")),
        P(None, ("seq", "vocab")),
        P(("groups", "seq")),
        P(("groups", "seq")),
    )
    return jax.shard_map(
        shards, mesh=mesh, in_specs=placed, out_specs=P(("groups", "seq", "vocab")), check_vma=False
    )
```

profile of v0, /device:TPU:0, one launch (start us, length us, event | category | flops | bytes accessed | tf_op | source)
XLA Modules:
  0.0 261.6 jit_solution(14560804017254880365)
XLA Ops:
  6.5 0.7 exponential_negate_fusion
  7.3 0.7 broadcast_multiply_fusion.2
  8.0 0.8 reshape.48
  8.9 0.1 broadcast_multiply_fusion
  9.0 2.3 fusion.23
  11.3 0.1 copy.30
  11.4 0.1 copy.33
  11.5 1.2 dynamic-slice
  12.8 1.3 dynamic-slice.2
  14.7 0.9 dynamic-update-slice.1
  15.5 0.8 dynamic-update-slice
  17.1 13.3 %all-reduce.5 = (s32[64]{0:T(128)S(1)}, s32[64]{0:T(128)S(1)}) all-reduce(s32[64]{0:T(128)S(1)} %dynamic-update-slice.1, s32[64]{0:T(128)S(1)} %dynamic-update-slice), channel_id=1, replica_groups=mesh['groups'=2,'seq'=8,'vocab'=2] {'seq'}, use_global_device_ids=true, to_apply=%add.1 | all-reduce | flops 128 | bytes 1024
  30.3 18.0 %all-gather.4 = f32[8,1,20]{2,1,0:T(1,128)S(1)} all-gather(f32[1,1,20]{2,1,0:T(1,128)S(1)} %get-tuple-element.339), channel_id=1, replica_groups=mesh['groups'=2,'seq'=8,'vocab'=2] {'seq'}, dimensions={0}, use_global_device_ids=true | all-gather | bytes 720 | tf_op jit(solution)/shard_map/all_gather | solution.py:9
  48.3 0.8 fusion.48
  49.2 0.4 convolution_bitcast_fusion.1
  49.5 51.0 %all-gather.8.cloned.1.call-done = f32[160,64,128]{2,1,0:T(8,128)} async-done(((f32[20,64,128]{2,1,0:T(8,128)}), f32[160,64,128]{2,1,0:T(8,128)}) %all-gather.8.cloned.1.call-update) | async-done | bytes 5242896 | tf_op jit(solution)/shard_map/all_gather | solution.py:9
  100.6 9.0 %while.34 = (s32[]{:T(128)}, f32[20,64,128]{2,1,0:T(8,128)S(1)}, s32[]{:T(128)}, f32[8,20]{1,0:T(8,128)S(1)}, f32[8,20,64,128]{3,2,1,0:T(8,128)}, /*index=5*/s32[]{:T(128)}, s32[]{:T(128)}) while((s32[]{:T(128)}, f32[20,64,128]{2,1,0:T(8,128)S(1)}, s32[]{:T(128)}, f32[8,20]{1,0:T(8,128)S(1)}, f32[8,20,64,128]{3,2,1,0:T(8,128)}, ...), condition=%wide.region_2.3_spmd.clone, body=%wide.region_1.2_spmd.clone.sunk | while | flops 655364 | bytes 1966433 | solution.py:18
  100.6 1.3 fusion.57
  101.9 1.2 fusion.57
  103.2 1.2 fusion.57
  104.5 1.2 fusion.57
  105.8 1.2 fusion.57
  107.0 1.2 fusion.57
  108.3 1.2 fusion.57
  109.6 0.9 fusion.10
  110.5 0.1 reshape.46
  110.6 30.6 %all_gather.45 = bf16[64,1280]{1,0:T(8,128)(2,1)S(1)} all-gather(bf16[8,1280]{1,0:T(8,128)(2,1)S(1)} %fusion.40), channel_id=1, replica_groups=mesh['groups'=2,'seq'=8,'vocab'=2] {'seq'}, dimensions={0}, use_global_device_ids=true | all-gather | bytes 184320 | tf_op jit(solution)/shard_map/all_gather | solution.py:92
  141.2 0.1 fusion.12
  141.4 2.5 psum.14
  143.8 1.0 fusion.18
  144.9 16.1 %all-reduce.9.cloned.1.call-done = f32[64,320]{1,0:T(8,128)} async-done(((f32[64,320]{1,0:T(8,128)}), f32[64,320]{1,0:T(8,128)}) %all-reduce.9.cloned.1.call-update) | async-done | bytes 81936 | tf_op jit(solution)/shard_map/psum | solution.py:102
  161.0 0.9 fusion.31
  161.9 31.4 %all-gather.5 = bf16[8,320,64]{1,2,0:T(8,128)(2,1)S(1)} all-gather(bf16[1,320,64]{1,2,0:T(8,128)(2,1)S(1)} %fusion.31), channel_id=1, replica_groups=mesh['groups'=2,'seq'=8,'vocab'=2] {'seq'}, dimensions={0}, use_global_device_ids=true | all-gather | bytes 368640 | tf_op jit(solution)/shard_map/all_gather | solution.py:104
  193.4 0.2 copy.37
  193.6 0.2 reshape.88
  193.8 0.1 multiply_reduce_fusion
  194.0 0.5 fusion.15
  194.5 0.3 select_reduce_fusion.1
  194.7 0.2 fusion.30
  195.0 0.2 dynamic-update-slice.2
  195.2 0.2 dynamic-update-slice.3
  195.4 0.2 dynamic-update-slice.4
  195.6 57.6 %all-reduce.6 = (f32[1024]{0:T(1024)S(1)}, f32[1024]{0:T(1024)S(1)}, f32[1024]{0:T(1024)S(1)}) all-reduce(f32[1024]{0:T(1024)S(1)} %dynamic-update-slice.2, f32[1024]{0:T(1024)S(1)} %dynamic-update-slice.3, f32[1024]{0:T(1024)S(1)} %dynamic-update-slice.4), channel_id=3, replica_groups=mesh['groups'=2,'seq'=8,'vocab'=2] {'seq','vocab'}, use_global_device_ids=true, to_apply=%add.2 | all-reduce | flops 3072 | bytes 24576
  253.3 0.1 reshape.50
  253.3 0.1 reshape.51
  253.4 0.1 reshape.52
  253.5 0.7 while.33
  254.2 0.6 dynamic_slice.60
  (63 shorter events, 0.7 us)
Async XLA Ops:
  6.5 187.4 %copy-start = (bf16[2560,196]{0,1:T(8,128)(2,1)S(1)}, bf16[2560,196]{0,1:T(8,128)(2,1)}, u32[]{:S(2)}) copy-start(bf16[2560,196]{0,1:T(8,128)(2,1)} %param.32) | copy-start | bytes 3010564
  6.5 94.0 %all-gather.8.cloned.1.call-start = ((), (), s32[]{:S(2)}) async-start(), calls=%async_computation.1 | async-start | bytes 5898240 | tf_op jit(solution)/shard_map/all_gather | solution.py:9
  11.3 98.3 %copy-start.6 = (bf16[8,128]{1,0:T(8,128)(2,1)S(1)}, bf16[8,128]{1,0:T(8,128)(2,1)}, u32[]{:S(2)}) copy-start(bf16[8,128]{1,0:T(8,128)(2,1)} %param.23) | copy-start | bytes 6148
  11.3 98.3 %copy-start.7 = (f32[20]{0:T(128)S(1)}, f32[20]{0:T(128)}, u32[]{:S(2)}) copy-start(f32[20]{0:T(128)} %param.27) | copy-start | bytes 244
  11.3 149.7 %all-reduce.9.cloned.1.call-start = ((), (), s32[]{:S(2)}) async-start(), calls=%async_computation | async-start | bytes 196608 | tf_op jit(solution)/shard_map/psum | solution.py:102
  100.6 10.0 %copy-start.3 = (bf16[8,1280]{1,0:T(8,128)(2,1)S(1)}, bf16[8,1280]{1,0:T(8,128)(2,1)}, u32[]{:S(2)}) copy-start(bf16[8,1280]{1,0:T(8,128)(2,1)} %param.21) | copy-start | bytes 61444
  100.6 43.3 %copy-start.1 = (bf16[1280,320]{0,1:T(8,128)(2,1)S(1)}, bf16[1280,320]{0,1:T(8,128)(2,1)}, u32[]{:S(2)}) copy-start(bf16[1280,320]{0,1:T(8,128)(2,1)} %param.29) | copy-start | bytes 2457604
  100.6 43.3 %copy-start.5 = (f32[1280]{0:T(1024)S(1)}, f32[1280]{0:T(1024)}, u32[]{:S(2)}) copy-start(f32[1280]{0:T(1024)} %param.28) | copy-start | bytes 15364
  100.6 60.5 %copy-start.2 = (bf16[64,320]{1,0:T(8,128)(2,1)S(1)}, bf16[64,320]{1,0:T(8,128)(2,1)}, u32[]{:S(2)}) copy-start(bf16[64,320]{1,0:T(8,128)(2,1)} %param.30) | copy-start | bytes 122884
  109.6 84.4 %copy-start.4 = (f32[2560]{0:T(1024)S(1)}, f32[2560]{0:T(1024)}, u32[]{:S(2)}) copy-start(f32[2560]{0:T(1024)} %param.31) | copy-start | bytes 30724
  109.6 84.9 %copy-start.8 = (s32[96,196]{1,0:T(8,128)S(1)}, s32[96,196]{1,0:T(8,128)}, u32[]{:S(2)}) copy-start(s32[96,196]{1,0:T(8,128)} %param.33) | copy-start | bytes 225796
Sparse Core Ops, SparseCore 0:
  11.4 89.1 all-gather.7
  145.0 15.9 all-reduce.8
where the time goes:
time: 262 us
  blocking collectives  153 us (58%)
  waiting for transfers between devices  67.2 us (26%)
  between operations  14.9 us (6%)
  other arithmetic  12.2 us (5%)
  local copies, waits for them, and re-layouts  7.35 us (3%)
  matrix products  6.07 us (2%)
    unnamed x2, blocking collectives  70.9 us
    all_gather x1, waiting for transfers between devices, carried_in(): pieces = jax.tree.map(lambda part: lax.all_gather(part, axis), value)  51 us
    all_gather x1, blocking collectives, shards(): full = lax.all_gather(hidden, 'seq', axis=1, tiled=True)  31.4 us
    all_gather x1, blocking collectives, shards(): lax.all_gather(gated, 'seq', axis=0, tiled=True)  30.6 us
    all_gather x1, blocking collectives, carried_in(): pieces = jax.tree.map(lambda part: lax.all_gather(part, axis), value)  18 us
    psum x1, waiting for transfers between devices, shards(): summed = lax.psum(partial_sum, 'vocab')  16.1 us
    select_n x7, other arithmetic, lap(): jnp.where(position < mine, new, old)  8.7 us
  transfers between devices with their start and end apart: 2, of which 2 were waited for; matrix products, arithmetic and copies ran while one was open for 2% of the time, Pallas kernels for 0%

commit v1 on v0

--- a/solution.py
+++ b/solution.py
@@ -99,7 +99,7 @@
     scale = lax.rsqrt(squares / (channels * pair_count) + 1e-05)
     normed = (every_f * scale[:, None] * norm_gain[None, :]).astype(jnp.bfloat16)
     partial_sum = jnp.dot(normed, out_weight, preferred_element_type=jnp.float32)
-    summed = lax.psum(partial_sum, "vocab")
+    summed = jnp.sum(lax.all_gather(partial_sum, "vocab"), axis=0)
     hidden = (residual.astype(jnp.float32) + summed).astype(jnp.bfloat16)
     full = lax.all_gather(hidden, "seq", axis=1, tiled=True)
     full_f = full.astype(jnp.float32)

time: 262 us -> 246 us (0.939)
  waiting for transfers between devices: 67.2 us -> 51.1 us
    psum x1 -> x0, waiting for transfers between devices: 16.1 us -> none  [shards(): summed = lax.psum(partial_sum, 'vocab')]
  transfers between devices with their start and end apart: 2 -> 1, of which waited for: 2 -> 1; matrix products, arithmetic and copies ran while one was open for 2% -> 2% of each run, Pallas kernels for 0% -> 0%
where the time goes in v1:
time: 246 us; the launch traced here: 245 us
  blocking collectives  155 us (63%)
  waiting for transfers between devices  51.1 us (21%)
  between operations  14.9 us (6%)
  other arithmetic  11.3 us (5%)
  local copies, waits for them, and re-layouts  7.35 us (3%)
  matrix products  5.43 us (2%)
    unnamed x2, blocking collectives  70.9 us
    all_gather x1, waiting for transfers between devices, carried_in(): pieces = jax.tree.map(lambda part: lax.all_gather(part, axis), value)  51.1 us
    all_gather x1, blocking collectives, shards(): full = lax.all_gather(hidden, 'seq', axis=1, tiled=True)  31 us
    all_gather x1, blocking collectives, shards(): lax.all_gather(gated, 'seq', axis=0, tiled=True)  30.6 us
    all_gather x1, blocking collectives, carried_in(): pieces = jax.tree.map(lambda part: lax.all_gather(part, axis), value)  18 us
    select_n x7, other arithmetic, lap(): jnp.where(position < mine, new, old)  8.7 us
    unnamed x31, local copies, waits for them, and re-layouts  4.98 us
  transfers between devices with their start and end apart: 1, of which 1 were waited for; matrix products, arithmetic and copies ran while one was open for 2% of the time, Pallas kernels for 0%

profile of v1, /device:TPU:0, one launch (start us, length us, event | category | flops | bytes accessed | tf_op | source)
XLA Modules:
  0.0 245.5 jit_solution(2076511855801569575)
XLA Ops:
  6.5 0.7 exponential_negate_fusion
  7.3 0.7 broadcast_multiply_fusion.2
  8.0 0.8 reshape.48
  8.9 0.1 broadcast_multiply_fusion
  9.0 2.3 fusion.23
  11.2 0.0 all-gather.9.cloned.1.call-update
  11.3 0.1 copy.30
  11.4 0.1 copy.33
  11.5 1.2 dynamic-slice
  12.7 1.3 dynamic-slice.2
  14.6 0.9 dynamic-update-slice.1
  15.5 0.8 dynamic-update-slice
  17.0 13.3 %all-reduce.5 = (s32[64]{0:T(128)S(1)}, s32[64]{0:T(128)S(1)}) all-reduce(s32[64]{0:T(128)S(1)} %dynamic-update-slice.1, s32[64]{0:T(128)S(1)} %dynamic-update-slice), channel_id=1, replica_groups=mesh['groups'=2,'seq'=8,'vocab'=2] {'seq'}, use_global_device_ids=true, to_apply=%add.1 | all-reduce | flops 128 | bytes 1024
  30.3 18.0 %all-gather.5 = f32[8,1,20]{2,1,0:T(1,128)S(1)} all-gather(f32[1,1,20]{2,1,0:T(1,128)S(1)} %get-tuple-element.339), channel_id=1, replica_groups=mesh['groups'=2,'seq'=8,'vocab'=2] {'seq'}, dimensions={0}, use_global_device_ids=true | all-gather | bytes 720 | tf_op jit(solution)/shard_map/all_gather | solution.py:9
  48.3 0.8 fusion.48
  49.1 0.3 convolution_bitcast_fusion.1
  49.5 51.1 %all-gather.9.cloned.1.call-done = f32[160,64,128]{2,1,0:T(8,128)} async-done(((f32[20,64,128]{2,1,0:T(8,128)}), f32[160,64,128]{2,1,0:T(8,128)}) %all-gather.9.cloned.1.call-update) | async-done | bytes 5242896 | tf_op jit(solution)/shard_map/all_gather | solution.py:9
  100.6 9.0 %while.34 = (s32[]{:T(128)}, f32[20,64,128]{2,1,0:T(8,128)S(1)}, s32[]{:T(128)}, f32[8,20]{1,0:T(8,128)S(1)}, f32[8,20,64,128]{3,2,1,0:T(8,128)}, /*index=5*/s32[]{:T(128)}, s32[]{:T(128)}) while((s32[]{:T(128)}, f32[20,64,128]{2,1,0:T(8,128)S(1)}, s32[]{:T(128)}, f32[8,20]{1,0:T(8,128)S(1)}, f32[8,20,64,128]{3,2,1,0:T(8,128)}, ...), condition=%wide.region_2.3_spmd.clone, body=%wide.region_1.2_spmd.clone.sunk | while | flops 655364 | bytes 1966433 | solution.py:18
  100.6 1.3 fusion.57
  101.9 1.2 fusion.57
  103.2 1.2 fusion.57
  104.5 1.2 fusion.57
  105.8 1.2 fusion.57
  107.0 1.2 fusion.57
  108.3 1.2 fusion.57
  109.6 0.9 fusion.10
  110.5 0.1 reshape.46
  110.6 30.6 %all_gather.51 = bf16[64,1280]{1,0:T(8,128)(2,1)S(1)} all-gather(bf16[8,1280]{1,0:T(8,128)(2,1)S(1)} %fusion.40), channel_id=1, replica_groups=mesh['groups'=2,'seq'=8,'vocab'=2] {'seq'}, dimensions={0}, use_global_device_ids=true | all-gather | bytes 184320 | tf_op jit(solution)/shard_map/all_gather | solution.py:92
  141.2 0.1 fusion.12
  141.4 2.5 %psum.7 = f32[64]{0:T(128)S(1)} all-reduce(f32[64]{0:T(128)S(1)} %fusion.12), channel_id=1, replica_groups=mesh['groups'=2,'seq'=8,'vocab'=2] {'vocab'}, use_global_device_ids=true, to_apply=%region_4.5 | all-reduce | flops 64 | bytes 512 | tf_op jit(solution)/shard_map/psum | solution.py:97
  143.8 0.4 fusion.18
  144.2 1.9 all-gather.1
  146.2 31.0 %all-gather.6 = bf16[8,320,64]{1,2,0:T(8,128)(2,1)S(1)} all-gather(bf16[1,320,64]{1,2,0:T(8,128)(2,1)S(1)} %fusion.31), channel_id=1, replica_groups=mesh['groups'=2,'seq'=8,'vocab'=2] {'seq'}, dimensions={0}, use_global_device_ids=true | all-gather | bytes 368640 | tf_op jit(solution)/shard_map/all_gather | solution.py:104
  177.2 0.2 copy.37
  177.5 0.2 reshape.89
  177.7 0.1 multiply_reduce_fusion
  177.9 0.5 fusion.15
  178.3 0.3 select_reduce_fusion.1
  178.6 0.2 fusion.30
  178.8 0.2 dynamic-update-slice.2
  179.1 0.2 dynamic-update-slice.3
  179.3 0.2 dynamic-update-slice.4
  179.5 57.6 %all-reduce.6 = (f32[1024]{0:T(1024)S(1)}, f32[1024]{0:T(1024)S(1)}, f32[1024]{0:T(1024)S(1)}) all-reduce(f32[1024]{0:T(1024)S(1)} %dynamic-update-slice.2, f32[1024]{0:T(1024)S(1)} %dynamic-update-slice.3, f32[1024]{0:T(1024)S(1)} %dynamic-update-slice.4), channel_id=4, replica_groups=mesh['groups'=2,'seq'=8,'vocab'=2] {'seq','vocab'}, use_global_device_ids=true, to_apply=%add.2 | all-reduce | flops 3072 | bytes 24576
  237.1 0.1 reshape.51
  237.2 0.1 reshape.52
  237.3 0.1 reshape.53
  237.4 0.7 while.33
  238.1 0.6 dynamic_slice.60
  (62 shorter events, 0.7 us)
Async XLA Ops:
  6.5 171.3 %copy-start = (bf16[2560,196]{0,1:T(8,128)(2,1)S(1)}, bf16[2560,196]{0,1:T(8,128)(2,1)}, u32[]{:S(2)}) copy-start(bf16[2560,196]{0,1:T(8,128)(2,1)} %param.32) | copy-start | bytes 3010564
  6.5 94.0 %all-gather.9.cloned.1.call-start = ((), (), s32[]{:S(2)}) async-start(), calls=%async_computation | async-start | bytes 5898240 | tf_op jit(solution)/shard_map/all_gather | solution.py:9
  11.3 98.3 %copy-start.6 = (bf16[8,128]{1,0:T(8,128)(2,1)S(1)}, bf16[8,128]{1,0:T(8,128)(2,1)}, u32[]{:S(2)}) copy-start(bf16[8,128]{1,0:T(8,128)(2,1)} %param.23) | copy-start | bytes 6148
  11.3 98.3 %copy-start.7 = (f32[20]{0:T(128)S(1)}, f32[20]{0:T(128)}, u32[]{:S(2)}) copy-start(f32[20]{0:T(128)} %param.27) | copy-start | bytes 244
  100.6 10.0 %copy-start.3 = (bf16[8,1280]{1,0:T(8,128)(2,1)S(1)}, bf16[8,1280]{1,0:T(8,128)(2,1)}, u32[]{:S(2)}) copy-start(bf16[8,1280]{1,0:T(8,128)(2,1)} %param.21) | copy-start | bytes 61444
  100.6 43.3 %copy-start.1 = (bf16[1280,320]{0,1:T(8,128)(2,1)S(1)}, bf16[1280,320]{0,1:T(8,128)(2,1)}, u32[]{:S(2)}) copy-start(bf16[1280,320]{0,1:T(8,128)(2,1)} %param.29) | copy-start | bytes 2457604
  100.6 43.3 %copy-start.5 = (f32[1280]{0:T(1024)S(1)}, f32[1280]{0:T(1024)}, u32[]{:S(2)}) copy-start(f32[1280]{0:T(1024)} %param.28) | copy-start | bytes 15364
  100.6 45.6 %copy-start.2 = (bf16[64,320]{1,0:T(8,128)(2,1)S(1)}, bf16[64,320]{1,0:T(8,128)(2,1)}, u32[]{:S(2)}) copy-start(bf16[64,320]{1,0:T(8,128)(2,1)} %param.30) | copy-start | bytes 122884
  109.6 68.3 %copy-start.4 = (f32[2560]{0:T(1024)S(1)}, f32[2560]{0:T(1024)}, u32[]{:S(2)}) copy-start(f32[2560]{0:T(1024)} %param.31) | copy-start | bytes 30724
  109.6 68.8 %copy-start.8 = (s32[96,196]{1,0:T(8,128)S(1)}, s32[96,196]{1,0:T(8,128)}, u32[]{:S(2)}) copy-start(s32[96,196]{1,0:T(8,128)} %param.33) | copy-start | bytes 225796
Sparse Core Ops, SparseCore 0:
  11.4 89.1 all-gather.8
